TPU v7x, 32 devices: a whole 2x2x4 slice. The times are simulated.
32 devices in a mesh: dp: 8 (over y, x, core), exch: 4 (over z).
Axes of the slice: x: 2, y: 2, z: 4, core: 2. Of those that a mesh axis runs over, the one named last changes fastest.
Arguments:
- x_raw: bfloat16 [1024, 2048], P('exch', 'dp'), may hold values from -6 to 6
- bc_raw: bfloat16 [1024, 256], P(('exch', 'dp')), may hold values from -6 to 6
- dt_raw: bfloat16 [32, 1024], P('dp', 'exch'), may hold values from -4 to 4
- cotangent: bfloat16 [1024, 2048], P('exch', 'dp'), may hold values from -6 to 6
- ssm_state: bfloat16 [8, 32, 64, 128], P('exch', 'dp'), may hold values from -0.625 to 0.625
- conv_x_state: bfloat16 [8, 3, 2048], P('exch', None, 'dp'), may hold values from -6 to 6
- conv_bc_state: bfloat16 [8, 3, 256], P('exch'), may hold values from -6 to 6
- owner: int32 [8], P('exch'), may hold values from 0 to 3, as said below
- resp_len: int32 [8], P('exch'), may hold values from 32 to 128, as said below
- conv_x_weight: float32 [4, 2048], P(None, 'dp'), may hold values from -3 to 3
- conv_bc_weight: float32 [4, 256], replicated, may hold values from -3 to 3
- dt_bias: float32 [32], P('dp'), may hold values from -5 to -3
- a_log: float32 [32], P('dp'), may hold values from -2.3 to 2.1
- skip_d: float32 [32], P('dp'), may hold values from 0.5 to 1.5
Outputs:
- grad_x: bfloat16 [1024, 2048], P('exch', 'dp')
- grad_bc: bfloat16 [1024, 256], P(('exch', 'dp'))
- grad_dt: bfloat16 [32, 1024], P('dp', 'exch')
- grad_conv_x: float32 [4, 2048], P(None, 'dp')
- grad_conv_bc: float32 [4, 256], replicated
- grad_heads: float32 [3, 32], P(None, 'dp')
Inputs may be any that keep to these rules, and one draw needn't show every extreme that they name: `owner`: among the 2 prompts of one holder (an aligned block along exch) no learner index occurs more than 1 times, and some learner index occurs exactly 1 times; over all 8 prompts every learner index occurs exactly 2 times. `resp_len`: every learner's block of 2 responses holds a response of length 128.
All inputs are finite; a program needn't handle non-finite values.
Results may differ from a plain program's by a relative error of at most 0.001.
Values may be sent and summed in bfloat16 or wider, within the bound.
A program may use at most 64 MiB of HBM per device.

v0:
```python
import jax
import jax.numpy as jnp
from jax import lax
from jax.sharding import PartitionSpec as P

DEV_GROUP = 8
SPAN = 128
GROUP = 1
CAP = 1
PRECISE = lax.Precision.HIGHEST


def conv_pre(raw, state, weight):
    padded = jnp.concatenate([state, raw], axis=1)
    length = raw.shape[1]
    total = padded[:, 0:length] * weight[0]
    for offset in range(1, weight.shape[0]):
        total = total + padded[:, offset : offset + length] * weight[offset]
    return total


def ssd_output(values, proj_b, proj_c, steps, rate, skip, start, block):
    rows, length, heads, width = values.shape
    count = length // block
    value_blocks = values.reshape(rows, count, block, heads, width)
    b_blocks = proj_b.reshape(rows, count, block, proj_b.shape[-1])
    c_blocks = proj_c.reshape(rows, count, block, proj_c.shape[-1])
    step_blocks = steps.reshape(rows, count, block, heads)
    logs = jnp.cumsum(-rate * step_blocks, axis=2)
    causal = jnp.tril(jnp.ones((block, block), jnp.float32))
    spread = logs[:, :, :, None, :] - logs[:, :, None, :, :]
    decays = jnp.exp(jnp.where(causal[:, :, None] > 0.5, spread, 0.0)) * causal[:, :, None]
    scores = jnp.einsum("rntk,rnsk->rnts", c_blocks, b_blocks, precision=PRECISE)
    weighted = value_blocks * step_blocks[..., None]
    mixing = scores[..., None] * decays
    intra = jnp.einsum("rntsh,rnshp->rnthp", mixing, weighted, precision=PRECISE)
    entry = jnp.exp(logs[:, 0])
    carried = jnp.einsum("rtk,rhpk->rthp", c_blocks[:, 0], start, precision=PRECISE)
    pieces = [carried * entry[..., None]]
    inter = jnp.stack(pieces, axis=1)
    output = intra + inter + skip[:, None] * value_blocks
    return output.reshape(rows, length, heads, width)


def window_loss(
    x_rows,
    bc_act,
    dt_rows,
    x_weight,
    bias,
    decay_log,
    skip,
    x_prev,
    start,
    cotan,
    mask,
    heads,
    block,
):
    x_act = jax.nn.silu(conv_pre(x_rows, x_prev, x_weight))
    rows, length, channels = x_rows.shape
    values = x_act.reshape(rows, length, heads, channels // heads)
    half = bc_act.shape[-1] // 2
    steps = jax.nn.softplus(dt_rows + bias)
    output = ssd_output(
        values,
        bc_act[..., :half],
        bc_act[..., half:],
        steps,
        jnp.exp(decay_log),
        skip,
        start,
        block,
    )
    return jnp.sum(output.reshape(rows, length, channels) * cotan * mask[..., None])


def local(
    x_raw,
    bc_raw,
    dt_raw,
    cotangent,
    ssm_state,
    conv_x_state,
    conv_bc_state,
    owner,
    resp_len,
    conv_x_weight,
    conv_bc_weight,
    dt_bias,
    a_log,
    skip_d,
):
    peer_count = lax.axis_size("exch")
    slices = lax.axis_size("dp")
    prompts = owner.shape[0]
    responses = resp_len.shape[0]
    head_count = dt_raw.shape[0]
    tokens = x_raw.shape[0]
    channels = x_raw.shape[1]
    pair_width = 2 * ssm_state.shape[-1]
    conv_depth = conv_x_state.shape[1]
    length = tokens // responses
    row_count = bc_raw.shape[0]
    groups = bc_raw.shape[1] // pair_width
    my_group = lax.axis_index("dp") // DEV_GROUP
    targets = jnp.arange(peer_count, dtype=jnp.int32)
    match = (owner[:, None] == targets[None, :]).astype(jnp.int32)
    earlier = jnp.cumsum(match, axis=0) - match
    places = jnp.sum(earlier * match, axis=1)
    slot_ids = jnp.arange(CAP, dtype=jnp.int32)
    routing = (match[:, :, None] == 1) & (places[:, None, None] == slot_ids[None, None, :])
    routing = routing.reshape(prompts, peer_count * CAP).astype(jnp.bfloat16)

    def pack_slots(values):
        moved = jnp.dot(routing.T, values.reshape(prompts, -1), preferred_element_type=jnp.float32)
        return moved.astype(jnp.bfloat16).reshape(peer_count, CAP, -1)

    bc_state = lax.dynamic_slice_in_dim(conv_bc_state, my_group * pair_width, pair_width, 2)
    filled = jnp.sum(routing, axis=0).reshape(peer_count, CAP)
    got_ssm, got_x, got_bc, got_fill = (
        lax.all_to_all(pack_slots(ssm_state), "exch", split_axis=0, concat_axis=0, tiled=True),
        lax.all_to_all(pack_slots(conv_x_state), "exch", split_axis=0, concat_axis=0, tiled=True),
        lax.all_to_all(pack_slots(bc_state), "exch", split_axis=0, concat_axis=0, tiled=True),
        lax.all_to_all(filled, "exch", split_axis=0, concat_axis=0, tiled=True),
    )
    present = (got_fill.reshape(peer_count * CAP) > 0.5).astype(jnp.int32)
    position = jnp.cumsum(present) - 1
    owned_ids = jnp.arange(prompts, dtype=jnp.int32)
    select = ((present[None, :] == 1) & (position[None, :] == owned_ids[:, None])).astype(
        jnp.bfloat16
    )

    def unpack(values, shape):
        chosen = jnp.dot(
            select, values.reshape(peer_count * CAP, -1), preferred_element_type=jnp.float32
        )
        return jnp.repeat(chosen, GROUP, axis=0).reshape(shape)

    start_state = unpack(got_ssm, (responses, head_count, channels // head_count, -1))
    x_prev = unpack(got_x, (responses, conv_depth, channels))
    bc_prev = unpack(got_bc, (responses, conv_depth, pair_width))
    gathered = lax.all_gather(bc_raw, "dp", axis=0, tiled=True)
    bc_local = lax.dynamic_slice_in_dim(gathered, my_group * pair_width, pair_width, 1)
    x_rows = x_raw.astype(jnp.float32).reshape(responses, length, channels)
    bc_rows = bc_local.astype(jnp.float32).reshape(responses, length, pair_width)
    cot_rows = cotangent.astype(jnp.float32).reshape(responses, length, channels)
    dt_rows = dt_raw.astype(jnp.float32).T.reshape(responses, length, head_count)
    live_mask = (jnp.arange(length, dtype=jnp.int32)[None, :] < resp_len[:, None]).astype(
        jnp.float32
    )
    bc_weight = lax.dynamic_slice_in_dim(conv_bc_weight, my_group * pair_width, pair_width, 1)
    bc_pre = conv_pre(bc_rows, bc_prev, bc_weight)
    bc_act, silu_back = jax.vjp(jax.nn.silu, bc_pre)

    def local_loss(x_in, bc_in, dt_in, x_weight, bias, decay_log, skip):
        return window_loss(
            x_in,
            bc_in,
            dt_in,
            x_weight,
            bias,
            decay_log,
            skip,
            x_prev,
            start_state,
            cot_rows,
            live_mask,
            head_count,
            SPAN,
        )

    grad_xr, grad_bca, grad_dtr, grad_wx, grad_bias, grad_decay, grad_skip = jax.grad(
        local_loss, argnums=(0, 1, 2, 3, 4, 5, 6)
    )(x_rows, bc_act, dt_rows, conv_x_weight, dt_bias, a_log, skip_d)
    grad_pre = silu_back(grad_bca)[0]
    unused, conv_back = jax.vjp(
        lambda raw, weight: conv_pre(raw, bc_prev, weight), bc_rows, bc_weight
    )
    grad_raw, grad_wbc = conv_back(grad_pre)
    returned = lax.all_to_all(
        grad_raw.reshape(slices, row_count, pair_width),
        "dp",
        split_axis=0,
        concat_axis=0,
        tiled=True,
    )
    grad_share = jnp.sum(returned.reshape(groups, DEV_GROUP, row_count, pair_width), axis=1)
    grad_share = grad_share.transpose(1, 0, 2).reshape(row_count, groups * pair_width)
    empty_taps = jnp.zeros((conv_depth + 1, groups * pair_width), jnp.float32)
    grad_wx, grad_bias, grad_decay, grad_skip = lax.psum(
        (grad_wx, grad_bias, grad_decay, grad_skip), "exch"
    )
    placed = lax.dynamic_update_slice_in_dim(empty_taps, grad_wbc, my_group * pair_width, 1)
    grad_taps = lax.psum(placed, ("dp", "exch"))
    grad_x = grad_xr.reshape(tokens, channels).astype(jnp.bfloat16)
    grad_bc = grad_share.astype(jnp.bfloat16)
    grad_dt = grad_dtr.reshape(tokens, head_count).T.astype(jnp.bfloat16)
    grad_heads = jnp.stack([grad_bias, grad_decay, grad_skip])
    return (grad_x, grad_bc, grad_dt, grad_wx, grad_taps, grad_heads)


def solution(mesh):
    in_specs = (
        P("exch", "dp"),
        P(("exch", "dp"), None),
        P("dp", "exch"),
        P("exch", "dp"),
        P("exch", "dp", None, None),
        P("exch", None, "dp"),
        P("exch", None, None),
        P("exch"),
        P("exch"),
        P(None, "dp"),
        P(),
        P("dp"),
        P("dp"),
        P("dp"),
    )
    out_specs = (
        P("exch", "dp"),
        P(("exch", "dp"), None),
        P("dp", "exch"),
        P(None, "dp"),
        P(),
        P(None, "dp"),
    )
    return jax.shard_map(local, mesh=mesh, in_specs=in_specs, out_specs=out_specs, check_vma=False)
```

profile of v0, /device:TPU:0, one launch (start us, length us, event | category | flops | bytes accessed | tf_op | source)
XLA Modules:
  0.0 124.4 jit_solution(9123671219750444243)
XLA Ops:
  0.6 0.7 fusion.80
  1.4 0.6 copy-done.8
  2.3 0.7 copy.167
  3.0 6.3 %all-to-all-start = ((bf16[4,1,1]{2,1,0:T(2,128)(2,1)}), bf16[4,1,1]{2,1,0:T(2,128)(2,1)S(1)}, u32[]{:S(2)}, u32[]{:S(2)}) async-start(bf16[4,1,1]{2,1,0:T(2,128)(2,1)} %copy.167), calls=%async_computation | async-start | bytes 4096 | tf_op jit(solution)/shard_map/all_to_all | solution.py:125
  9.4 1.2 reshape.547
  10.7 0.2 reshape.548
  10.9 0.4 copy-done.13
  11.4 0.6 copy-done.3
  12.2 0.6 copy-done.6
  12.8 0.7 copy-done.7
  13.6 0.5 broadcast.324
  14.2 0.7 reduce.16
  14.8 0.6 reshape.551
  15.7 0.7 reduce.17
  16.4 0.6 reshape.553
  17.4 0.6 copy-done.4
  18.1 9.3 %all_gather.3 = bf16[256,256]{1,0:T(8,128)(2,1)S(1)} all-gather(bf16[32,256]{1,0:T(8,128)(2,1)S(1)} %copy-done.4), channel_id=1, replica_groups=mesh['dp'=8,'exch'=4] {'dp'}, dimensions={0}, use_global_device_ids=true | all-gather | bytes 147456 | tf_op jit(solution)/shard_map/all_gather | solution.py:143
  27.5 0.4 fusion
  27.8 1.0 reduce.18
  28.8 1.0 reshape.555
  29.8 0.9 copy-done.2
  31.1 5.1 %all-to-all-start.1 = ((bf16[4,2,384]{2,1,0:T(2,128)(2,1)}), bf16[4,2,384]{2,1,0:T(2,128)(2,1)S(1)}, u32[]{:S(2)}, u32[]{:S(2)}) async-start(bf16[4,2,384]{2,1,0:T(2,128)(2,1)} %reshape.553), calls=%async_computation.1 | async-start | bytes 12288 | tf_op jit(solution)/shard_map/all_to_all | solution.py:124
  36.6 5.2 %all-to-all-done.1 = bf16[4,2,384]{2,1,0:T(2,128)(2,1)S(1)} async-done(((bf16[4,2,384]{2,1,0:T(2,128)(2,1)}), bf16[4,2,384]{2,1,0:T(2,128)(2,1)S(1)}, u32[]{:S(2)}, u32[]{:S(2)}) %all-to-all-start.1) | async-done | bytes 6176 | tf_op jit(solution)/shard_map/all_to_all | solution.py:124
  41.8 3.2 %all-to-all-start.2 = ((bf16[4,2,384]{2,1,0:T(2,128)(2,1)}), bf16[4,2,384]{2,1,0:T(2,128)(2,1)S(1)}, u32[]{:S(2)}, u32[]{:S(2)}) async-start(bf16[4,2,384]{2,1,0:T(2,128)(2,1)} %reshape.551), calls=%async_computation.2 | async-start | bytes 12288 | tf_op jit(solution)/shard_map/all_to_all | solution.py:123
  45.3 5.4 %all-to-all-done.2 = bf16[4,2,384]{2,1,0:T(2,128)(2,1)S(1)} async-done(((bf16[4,2,384]{2,1,0:T(2,128)(2,1)}), bf16[4,2,384]{2,1,0:T(2,128)(2,1)S(1)}, u32[]{:S(2)}, u32[]{:S(2)}) %all-to-all-start.2) | async-done | bytes 6176 | tf_op jit(solution)/shard_map/all_to_all | solution.py:123
  50.6 3.4 %all-to-all-start.3 = ((bf16[4,2,16384]{2,1,0:T(2,128)(2,1)}), bf16[4,2,16384]{2,1,0:T(2,128)(2,1)S(1)}, u32[]{:S(2)}, u32[]{:S(2)}) async-start(bf16[4,2,16384]{2,1,0:T(2,128)(2,1)} %reshape.555), calls=%async_computation.3 | async-start | bytes 524288 | tf_op jit(solution)/shard_map/all_to_all | solution.py:122
  54.9 0.4 fusion.46
  55.3 1.3 %fusion.10 = (f32[2,128,4]{1,2,0:T(4,128)S(1)}, f32[2,128,4]{1,2,0:T(4,128)S(1)}, f32[2,128,128]{2,1,0:T(8,128)S(1)}) fusion(f32[2,128,128]{2,1,0:T(8,128)S(1)} %fusion.46, f32[128,128]{1,0:T(8,128)S(1)} %fusion.52, f32[2,128,4]{1,2,0:T(4,128)S(1)} %copy.171, pred[128,128]{1,0:T(8,128)(4,1)S(1)} %broadcast_compare_fusion, ...), kind=kOutput, calls=%fused_computation.27 | convolution fusion | flops 102201344 | bytes 885760 | tf_op jit(solution)/shard_map/transpose(jvp(rntsh,rnshp->rnthp))/dot_general | solution.py:36
  56.6 0.7 copy-done.12
  57.3 0.8 multiply_reduce_fusion.10
  59.0 0.7 fusion.19
  59.8 0.4 fusion.49
  60.2 0.6 all-to-all-done.3
  60.8 0.3 reshape.556
  61.0 0.3 copy.204
  61.4 0.3 fusion.72
  61.7 0.4 fusion.1
  62.1 0.6 convolution_bitcast_fusion.2
  62.9 0.3 convolution_add_fusion
  63.2 0.2 multiply_reduce_fusion.4
  63.4 39.4 %psum.36 = f32[4,256]{1,0:T(4,128)} all-reduce(f32[4,256]{1,0:T(4,128)S(1)} %pad_add_fusion.6), channel_id=1, replica_groups=mesh['dp'=8,'exch'=4] {'dp','exch'}, use_global_device_ids=true, to_apply=%region_21.22 | all-reduce | flops 1024 | bytes 8192 | tf_op jit(solution)/shard_map/psum | solution.py:195
  102.9 2.2 %reduce_window_sum.46 = f32[2,1,128,4]{3,2,1,0:T(8,128)S(1)} reduce-window(f32[2,1,128,4]{3,2,1,0:T(8,128)S(1)} %bitcast_add_fusion, f32[]{:T(128)} %constant.56.clone.1), window={size=1x1x128x1 pad=0_0x0_0x0_127x0_0}, to_apply=%region_11.12 | reduce-window | flops 130048 | bytes 8196 | tf_op jit(solution)/shard_map/transpose(jvp(jit(cumsum)))/reduce_window_sum | solution.py:29
  105.2 0.8 multiply_reduce_fusion.11
  106.1 0.8 pad_add_fusion
  106.9 4.8 %all-to-all-start.4 = ((f32[8,32,256]{2,1,0:T(8,128)}), f32[8,32,256]{2,1,0:T(8,128)S(1)}, u32[]{:S(2)}, u32[]{:S(2)}) async-start(f32[8,32,256]{2,1,0:T(8,128)} %bitcast.44), calls=%async_computation.4 | async-start | bytes 524288 | tf_op jit(solution)/shard_map/all_to_all | solution.py:181
  111.9 11.3 %all-reduce.18 = (f32[4,256]{1,0:T(4,128)}, f32[1,4]{1,0:T(1,128)S(1)}, f32[1,4]{1,0:T(1,128)S(1)}, f32[1,4]{1,0:T(1,128)S(1)}) all-reduce(f32[4,256]{1,0:T(4,128)S(1)} %pad_add_fusion.7, f32[1,4]{1,0:T(1,128)S(1)} %bitcast.233, f32[1,4]{1,0:T(1,128)S(1)} %multiply_bitcast_fusion, ...), channel_id=1, replica_groups=mesh['dp'=8,'exch'=4] {'exch'}, use_global_device_ids=true, to_apply=%region_16.17 | all-reduce | flops 1036 | bytes 8288 | tf_op jit(solution)/shard_map/psum | solution.py:191
  123.2 0.6 pad_maximum_fusion.2
  123.8 0.6 reduce_sum.196
  (77 shorter events, 5.0 us)
Async XLA Ops:
  0.6 12.8 %copy-start = (bf16[2,3,256]{2,0,1:T(2,128)(2,1)S(1)}, bf16[2,3,256]{2,0,1:T(2,128)(2,1)}, u32[]{:S(2)}) copy-start(bf16[2,3,256]{2,0,1:T(2,128)(2,1)} %param.19) | copy-start | bytes 9220
  1.4 0.7 copy-start.8
  3.0 28.1 %all-to-all-start = ((bf16[4,1,1]{2,1,0:T(2,128)(2,1)}), bf16[4,1,1]{2,1,0:T(2,128)(2,1)S(1)}, u32[]{:S(2)}, u32[]{:S(2)}) async-start(bf16[4,1,1]{2,1,0:T(2,128)(2,1)} %copy.167), calls=%async_computation | async-start | bytes 4096 | tf_op jit(solution)/shard_map/all_to_all | solution.py:125
  9.4 1.2 copy-start.1
  10.6 0.7 copy-start.13
  10.7 0.7 copy-start.11
  11.3 0.7 copy-start.3
  11.3 0.7 copy-start.5
  12.1 0.7 copy-start.6
  12.8 0.7 copy-start.7
  14.8 0.7 copy-start.10
  17.3 0.7 copy-start.4
  18.0 9.4 %copy-start.9 = (bf16[2,4,64,128]{3,2,1,0:T(8,128)(2,1)S(1)}, bf16[2,4,64,128]{3,2,1,0:T(8,128)(2,1)}, u32[]{:S(2)}) copy-start(bf16[2,4,64,128]{3,2,1,0:T(8,128)(2,1)} %param.18) | copy-start | bytes 393220
  29.8 0.9 copy-start.2
  31.1 10.7 %all-to-all-start.1 = ((bf16[4,2,384]{2,1,0:T(2,128)(2,1)}), bf16[4,2,384]{2,1,0:T(2,128)(2,1)S(1)}, u32[]{:S(2)}, u32[]{:S(2)}) async-start(bf16[4,2,384]{2,1,0:T(2,128)(2,1)} %reshape.553), calls=%async_computation.1 | async-start | bytes 12288 | tf_op jit(solution)/shard_map/all_to_all | solution.py:124
  41.8 8.8 %all-to-all-start.2 = ((bf16[4,2,384]{2,1,0:T(2,128)(2,1)}), bf16[4,2,384]{2,1,0:T(2,128)(2,1)S(1)}, u32[]{:S(2)}, u32[]{:S(2)}) async-start(bf16[4,2,384]{2,1,0:T(2,128)(2,1)} %reshape.551), calls=%async_computation.2 | async-start | bytes 12288 | tf_op jit(solution)/shard_map/all_to_all | solution.py:123
  50.6 10.2 %all-to-all-start.3 = ((bf16[4,2,16384]{2,1,0:T(2,128)(2,1)}), bf16[4,2,16384]{2,1,0:T(2,128)(2,1)S(1)}, u32[]{:S(2)}, u32[]{:S(2)}) async-start(bf16[4,2,16384]{2,1,0:T(2,128)(2,1)} %reshape.555), calls=%async_computation.3 | async-start | bytes 524288 | tf_op jit(solution)/shard_map/all_to_all | solution.py:122
  56.6 0.7 copy-start.12
  106.9 16.9 %all-to-all-start.4 = ((f32[8,32,256]{2,1,0:T(8,128)}), f32[8,32,256]{2,1,0:T(8,128)S(1)}, u32[]{:S(2)}, u32[]{:S(2)}) async-start(f32[8,32,256]{2,1,0:T(8,128)} %bitcast.44), calls=%async_computation.4 | async-start | bytes 524288 | tf_op jit(solution)/shard_map/all_to_all | solution.py:181
where the time goes:
time: 125 us; the launch traced here: 124 us
  blocking collectives  60.1 us (48%)
  starting transfers between devices  22.9 us (18%)
  local copies, waits for them, and re-layouts  12.2 us (10%)
  other arithmetic  11.7 us (9%)
  waiting for transfers between devices  11.2 us (9%)
  matrix products  5.42 us (4%)
    psum x1, blocking collectives, local(): grad_taps = lax.psum(placed, ('dp', 'exch'))  39.4 us
    psum x1, blocking collectives, local(): lax.psum((grad_wx, grad_bias, grad_decay, grad_skip), 'exch')  11.3 us
    all_gather x1, blocking collectives, local(): gathered = lax.all_gather(bc_raw, 'dp', axis=0, tiled=True)  9.34 us
    unnamed x37, local copies, waits for them, and re-layouts  7.99 us
    all_to_all x1, starting transfers between devices, local(): lax.all_to_all(filled, 'exch', split_axis=0, concat_axis=0, tiled=True)  6.35 us
    all_to_all x1, waiting for transfers between devices, local(): lax.all_to_all(pack_slots(conv_x_state), 'exch', split_axis=0, concat_axi...  5.35 us
    all_to_all x1, waiting for transfers between devices, local(): lax.all_to_all(pack_slots(bc_state), 'exch', split_axis=0, concat_axis=0,...  5.23 us
    all_to_all x1, starting transfers between devices, local(): lax.all_to_all(pack_slots(bc_state), 'exch', split_axis=0, concat_axis=0,...  5.11 us
  transfers between devices with their start and end apart: 5, of which 3 were waited for; matrix products, arithmetic and copies ran while one was open for 12% of the time, Pallas kernels for 0%

commit v1 on v0

--- a/solution.py
+++ b/solution.py
@@ -192,7 +192,7 @@
         (grad_wx, grad_bias, grad_decay, grad_skip), "exch"
     )
     placed = lax.dynamic_update_slice_in_dim(empty_taps, grad_wbc, my_group * pair_width, 1)
-    grad_taps = lax.psum(placed, ("dp", "exch"))
+    grad_taps = lax.psum(lax.psum(placed, "exch"), "dp")
     grad_x = grad_xr.reshape(tokens, channels).astype(jnp.bfloat16)
     grad_bc = grad_share.astype(jnp.bfloat16)
     grad_dt = grad_dtr.reshape(tokens, head_count).T.astype(jnp.bfloat16)

time: 125 us -> 105 us (0.84)
  blocking collectives: 60.1 us -> 35.1 us
  local copies, waits for them, and re-layouts: 12.2 us -> 17.2 us
    psum x1, blocking collectives: 39.4 us -> 12.9 us  [local(): grad_taps = lax.psum(lax.psum(placed, 'exch'), 'dp')]
    unnamed x37 -> x99, local copies, waits for them, and re-layouts: 7.99 us -> 12.4 us
    psum x1, blocking collectives: 11.3 us -> 12.9 us  [local(): lax.psum((grad_wx, grad_bias, grad_decay, grad_skip), 'exch')]
    all_to_all x1, starting transfers between devices: 4.78 us -> 3.41 us  [local(): lax.all_to_all(grad_raw.reshape(slices, row_count, pair_width), 'dp', spl...]
  transfers between devices with their start and end apart: 5 -> 5, of which waited for: 3 -> 2; matrix products, arithmetic and copies ran while one was open for 12% -> 16% of each run, Pallas kernels for 0% -> 0%
where the time goes in v1:
time: 105 us; the launch traced here: 104 us
  blocking collectives  35.1 us (33%)
  starting transfers between devices  21.7 us (21%)
  local copies, waits for them, and re-layouts  17.2 us (16%)
  other arithmetic  12.2 us (12%)
  waiting for transfers between devices  10.6 us (10%)
  matrix products  5.99 us (6%)
  between operations  1.3 us (1%)
    psum x1, blocking collectives, local(): grad_taps = lax.psum(lax.psum(placed, 'exch'), 'dp')  12.9 us
    psum x1, blocking collectives, local(): lax.psum((grad_wx, grad_bias, grad_decay, grad_skip), 'exch')  12.9 us
    unnamed x99, local copies, waits for them, and re-layouts  12.4 us
    all_gather x1, blocking collectives, local(): gathered = lax.all_gather(bc_raw, 'dp', axis=0, tiled=True)  9.34 us
    all_to_all x1, starting transfers between devices, local(): lax.all_to_all(filled, 'exch', split_axis=0, concat_axis=0, tiled=True)  6.35 us
    all_to_all x1, waiting for transfers between devices, local(): lax.all_to_all(pack_slots(conv_x_state), 'exch', split_axis=0, concat_axi...  5.35 us
    all_to_all x1, waiting for transfers between devices, local(): lax.all_to_all(pack_slots(bc_state), 'exch', split_axis=0, concat_axis=0,...  5.23 us
    all_to_all x1, starting transfers between devices, local(): lax.all_to_all(pack_slots(bc_state), 'exch', split_axis=0, concat_axis=0,...  5.1 us
  transfers between devices with their start and end apart: 5, of which 2 were waited for; matrix products, arithmetic and copies ran while one was open for 16% of the time, Pallas kernels for 0%

profile of v1, /device:TPU:0, one launch (start us, length us, event | category | flops | bytes accessed | tf_op | source)
XLA Modules:
  0.0 104.1 jit_solution(4896721034220120818)
XLA Ops:
  0.6 0.7 fusion.80
  1.4 0.6 copy-done.34
  2.3 0.7 copy.167
  3.0 6.3 %all-to-all-start = ((bf16[4,1,1]{2,1,0:T(2,128)(2,1)}), bf16[4,1,1]{2,1,0:T(2,128)(2,1)S(1)}, u32[]{:S(2)}, u32[]{:S(2)}) async-start(bf16[4,1,1]{2,1,0:T(2,128)(2,1)} %copy.167), calls=%async_computation | async-start | bytes 4096 | tf_op jit(solution)/shard_map/all_to_all | solution.py:125
  9.4 1.2 %reshape.547 = f32[2,1,128,4,64]{4,3,2,0,1:T(4,128)S(1)} reshape(bf16[256,256]{1,0:T(8,128)(2,1)} %param.17) | data formatting | bytes 393216 | tf_op jit(solution)/shard_map/reshape | solution.py:147
  10.9 0.4 copy-done.43
  11.4 0.6 copy-done.7
  12.2 0.6 copy-done.30
  12.8 0.7 copy-done.31
  13.7 0.5 broadcast.324
  14.2 0.7 reduce.16
  14.9 0.6 reshape.551
  15.8 0.7 reduce.17
  16.4 0.6 reshape.553
  17.5 0.6 copy-done.9
  18.1 9.3 %all_gather.3 = bf16[256,256]{1,0:T(8,128)(2,1)S(1)} all-gather(bf16[32,256]{1,0:T(8,128)(2,1)S(1)} %copy-done.9), channel_id=1, replica_groups=mesh['dp'=8,'exch'=4] {'dp'}, dimensions={0}, use_global_device_ids=true | all-gather | bytes 147456 | tf_op jit(solution)/shard_map/all_gather | solution.py:143
  27.5 0.7 copy.179
  28.5 1.0 reduce.18
  29.5 1.0 reshape.555
  30.5 0.9 copy-done.2
  31.8 5.1 %all-to-all-start.1 = ((bf16[4,2,384]{2,1,0:T(2,128)(2,1)}), bf16[4,2,384]{2,1,0:T(2,128)(2,1)S(1)}, u32[]{:S(2)}, u32[]{:S(2)}) async-start(bf16[4,2,384]{2,1,0:T(2,128)(2,1)} %reshape.553), calls=%async_computation.1 | async-start | bytes 12288 | tf_op jit(solution)/shard_map/all_to_all | solution.py:124
  37.2 5.2 %all-to-all-done.1 = bf16[4,2,384]{2,1,0:T(2,128)(2,1)S(1)} async-done(((bf16[4,2,384]{2,1,0:T(2,128)(2,1)}), bf16[4,2,384]{2,1,0:T(2,128)(2,1)S(1)}, u32[]{:S(2)}, u32[]{:S(2)}) %all-to-all-start.1) | async-done | bytes 6176 | tf_op jit(solution)/shard_map/all_to_all | solution.py:124
  42.5 3.2 %all-to-all-start.2 = ((bf16[4,2,384]{2,1,0:T(2,128)(2,1)}), bf16[4,2,384]{2,1,0:T(2,128)(2,1)S(1)}, u32[]{:S(2)}, u32[]{:S(2)}) async-start(bf16[4,2,384]{2,1,0:T(2,128)(2,1)} %reshape.551), calls=%async_computation.2 | async-start | bytes 12288 | tf_op jit(solution)/shard_map/all_to_all | solution.py:123
  45.9 5.3 %all-to-all-done.2 = bf16[4,2,384]{2,1,0:T(2,128)(2,1)S(1)} async-done(((bf16[4,2,384]{2,1,0:T(2,128)(2,1)}), bf16[4,2,384]{2,1,0:T(2,128)(2,1)S(1)}, u32[]{:S(2)}, u32[]{:S(2)}) %all-to-all-start.2) | async-done | bytes 6176 | tf_op jit(solution)/shard_map/all_to_all | solution.py:123
  51.3 3.6 %all-to-all-start.3 = ((bf16[4,2,16384]{2,1,0:T(2,128)(2,1)}), bf16[4,2,16384]{2,1,0:T(2,128)(2,1)S(1)}, u32[]{:S(2)}, u32[]{:S(2)}) async-start(bf16[4,2,16384]{2,1,0:T(2,128)(2,1)} %reshape.555), calls=%async_computation.3 | async-start | bytes 524288 | tf_op jit(solution)/shard_map/all_to_all | solution.py:122
  55.2 0.8 multiply_reduce_fusion.1
  56.4 0.4 fusion.46
  56.8 0.6 copy-done.42
  57.5 1.4 %multiply_reduce_fusion.10 = (f32[2,128,4]{1,2,0:T(4,128)}, f32[2,1,128,4,64]{2,4,3,0,1:T(8,128)S(1)}) fusion(f32[2,1,128,4,64]{2,4,3,0,1:T(8,128)S(1)} %bitcast.201, f32[2,128,4]{1,2,0:T(4,128)S(1)} %compare_select_fusion.5, f32[2,1,128,4,64]{2,4,3,0,1:T(8,128)S(1)} %copy.166, f32[2,128]{1,0:T(2,128)S(1)} %compare_convert_fusion.1, f32[4]{0:T(128)S(1)} %copy-done.42, ...), kind=kOutput, calls=%fused_computation.60 | convolution fusion | flops 101645312 | bytes 1012752 | tf_op jit(solution)/shard_map/transpose(jvp(rntsh,rnshp->rnthp))/dot_general | solution.py:36
  59.4 0.7 copy-done.4
  60.1 1.3 %fusion.10 = (f32[2,128,4]{1,2,0:T(4,128)S(1)}, f32[2,128,4]{1,2,0:T(4,128)S(1)}, f32[2,128,128]{2,1,0:T(8,128)S(1)}) fusion(f32[2,128,128]{2,1,0:T(8,128)S(1)} %copy-done.4, f32[128,128]{1,0:T(8,128)S(1)} %copy-done.6, f32[2,128,4]{1,2,0:T(4,128)S(1)} %copy-done.29, pred[128,128]{1,0:T(8,128)(4,1)S(1)} %copy-done.12, f32[2,128,4,64]{1,3,2,0:T(8,128)S(1)} %bitcast.202, ...), kind=kOutput, calls=%fused_computation.27 | convolution fusion | flops 102201344 | bytes 885760 | tf_op jit(solution)/shard_map/transpose(jvp(rntsh,rnshp->rnthp))/dot_general | solution.py:36
  61.4 0.7 copy-done.27
  62.6 0.7 fusion.19
  63.4 0.4 fusion.49
  64.4 0.7 copy-done.36
  65.4 0.4 fusion.1
  66.0 0.6 convolution_bitcast_fusion.2
  67.2 2.2 %reduce_window_sum.46 = f32[2,1,128,4]{3,2,1,0:T(8,128)S(1)} reduce-window(f32[2,1,128,4]{3,2,1,0:T(8,128)S(1)} %bitcast_add_fusion, f32[]{:T(128)} %constant.56.clone.1), window={size=1x1x128x1 pad=0_0x0_0x0_127x0_0}, to_apply=%region_11.12 | reduce-window | flops 130048 | bytes 8196 | tf_op jit(solution)/shard_map/transpose(jvp(jit(cumsum)))/reduce_window_sum | solution.py:29
  69.5 0.6 copy-done.10
  70.2 0.8 multiply_reduce_fusion.11
  71.0 0.7 copy-done.44
  72.2 0.4 copy-done.18
  72.9 0.8 pad_add_fusion
  73.6 3.4 %all-to-all-start.4 = ((f32[8,32,256]{2,1,0:T(8,128)}), f32[8,32,256]{2,1,0:T(8,128)S(1)}, u32[]{:S(2)}, u32[]{:S(2)}) async-start(f32[8,32,256]{2,1,0:T(8,128)} %bitcast.44), calls=%async_computation.4 | async-start | bytes 524288 | tf_op jit(solution)/shard_map/all_to_all | solution.py:181
  77.1 12.9 %all-reduce.18 = (f32[4,256]{1,0:T(4,128)}, f32[4,256]{1,0:T(4,128)S(1)}, f32[1,4]{1,0:T(1,128)S(1)}, f32[1,4]{1,0:T(1,128)S(1)}, f32[1,4]{1,0:T(1,128)S(1)}) all-reduce(f32[4,256]{1,0:T(4,128)S(1)} %get-tuple-element.51, f32[4,256]{1,0:T(4,128)S(1)} %get-tuple-element.50, ...), channel_id=1, replica_groups=mesh['dp'=8,'exch'=4] {'exch'}, use_global_device_ids=true, to_apply=%region_16.17 | all-reduce | flops 2060 | bytes 16480 | tf_op jit(solution)/shard_map/psum | solution.py:191
  90.0 12.9 %psum.44 = f32[4,256]{1,0:T(4,128)} all-reduce(f32[4,256]{1,0:T(4,128)S(1)} %get-tuple-element.18), channel_id=1, replica_groups=mesh['dp'=8,'exch'=4] {'dp'}, use_global_device_ids=true, to_apply=%region_22.23 | all-reduce | flops 1024 | bytes 8192 | tf_op jit(solution)/shard_map/psum | solution.py:195
  102.9 0.6 pad_maximum_fusion.2
  103.4 0.6 reduce_sum.196
  (138 shorter events, 7.4 us)
Async XLA Ops:
  0.6 12.9 %copy-start = (bf16[2,3,256]{2,0,1:T(2,128)(2,1)S(1)}, bf16[2,3,256]{2,0,1:T(2,128)(2,1)}, u32[]{:S(2)}) copy-start(bf16[2,3,256]{2,0,1:T(2,128)(2,1)} %param.19) | copy-start | bytes 9220
  1.4 0.7 copy-start.34
  3.0 28.8 %all-to-all-start = ((bf16[4,1,1]{2,1,0:T(2,128)(2,1)}), bf16[4,1,1]{2,1,0:T(2,128)(2,1)S(1)}, u32[]{:S(2)}, u32[]{:S(2)}) async-start(bf16[4,1,1]{2,1,0:T(2,128)(2,1)} %copy.167), calls=%async_computation | async-start | bytes 4096 | tf_op jit(solution)/shard_map/all_to_all | solution.py:125
  9.4 47.4 %copy-start.11 = (pred[128,128]{1,0:T(8,128)(4,1)}, pred[128,128]{1,0:T(8,128)(4,1)S(1)}, u32[]{:S(2)}) copy-start(pred[128,128]{1,0:T(8,128)(4,1)S(1)} %broadcast_compare_fusion) | copy-start | bytes 49156
  9.4 47.4 %copy-start.5 = (f32[128,128]{1,0:T(8,128)}, f32[128,128]{1,0:T(8,128)S(1)}, u32[]{:S(2)}) copy-start(f32[128,128]{1,0:T(8,128)S(1)} %fusion.52) | copy-start | bytes 196612
  9.4 1.2 %copy-start.1 = (bf16[256,256]{1,0:T(8,128)(2,1)S(1)}, bf16[256,256]{1,0:T(8,128)(2,1)}, u32[]{:S(2)}) copy-start(bf16[256,256]{1,0:T(8,128)(2,1)} %param.17) | copy-start | bytes 393220
  10.7 0.7 copy-start.43
  10.7 0.7 copy-start.41
  11.3 0.7 copy-start.7
  11.3 0.8 copy-start.25
  11.3 0.7 copy-start.23
  12.0 44.8 %copy-start.13 = (f32[2,128]{1,0:T(2,128)}, f32[2,128]{1,0:T(2,128)S(1)}, u32[]{:S(2)}) copy-start(f32[2,128]{1,0:T(2,128)S(1)} %compare_convert_fusion.1) | copy-start | bytes 3076
  12.1 44.7 %copy-start.32 = (f32[2,128,4]{1,2,0:T(4,128)}, f32[2,128,4]{1,2,0:T(4,128)S(1)}, u32[]{:S(2)}) copy-start(f32[2,128,4]{1,2,0:T(4,128)S(1)} %compare_select_fusion.5) | copy-start | bytes 12292
  12.1 0.7 copy-start.30
  12.8 0.7 copy-start.31
  13.5 42.7 %copy-start.15 = (f32[1,256]{1,0:T(1,128)}, f32[1,256]{1,0:T(1,128)S(1)}, u32[]{:S(2)}) copy-start(f32[1,256]{1,0:T(1,128)S(1)} %get-tuple-element.42) | copy-start | bytes 3076
  13.5 42.7 %copy-start.17 = (f32[1,256]{1,0:T(1,128)}, f32[1,256]{1,0:T(1,128)S(1)}, u32[]{:S(2)}) copy-start(f32[1,256]{1,0:T(1,128)S(1)} %get-tuple-element.43) | copy-start | bytes 3076
  13.5 42.7 %copy-start.19 = (f32[1,256]{1,0:T(1,128)}, f32[1,256]{1,0:T(1,128)S(1)}, u32[]{:S(2)}) copy-start(f32[1,256]{1,0:T(1,128)S(1)} %get-tuple-element.44) | copy-start | bytes 3076
  13.5 42.7 %copy-start.21 = (f32[1,256]{1,0:T(1,128)}, f32[1,256]{1,0:T(1,128)S(1)}, u32[]{:S(2)}) copy-start(f32[1,256]{1,0:T(1,128)S(1)} %get-tuple-element.45) | copy-start | bytes 3076
  14.9 0.7 copy-start.40
  17.4 0.7 copy-start.9
  18.1 38.7 %copy-start.28 = (f32[2,128,4]{1,2,0:T(4,128)}, f32[2,128,4]{1,2,0:T(4,128)S(1)}, u32[]{:S(2)}) copy-start(f32[2,128,4]{1,2,0:T(4,128)S(1)} %copy.171) | copy-start | bytes 12292
  18.1 10.0 %copy-start.39 = (bf16[2,4,64,128]{3,2,1,0:T(8,128)(2,1)S(1)}, bf16[2,4,64,128]{3,2,1,0:T(8,128)(2,1)}, u32[]{:S(2)}) copy-start(bf16[2,4,64,128]{3,2,1,0:T(8,128)(2,1)} %param.18) | copy-start | bytes 393220
  30.5 0.9 copy-start.2
  31.8 10.7 %all-to-all-start.1 = ((bf16[4,2,384]{2,1,0:T(2,128)(2,1)}), bf16[4,2,384]{2,1,0:T(2,128)(2,1)S(1)}, u32[]{:S(2)}, u32[]{:S(2)}) async-start(bf16[4,2,384]{2,1,0:T(2,128)(2,1)} %reshape.553), calls=%async_computation.1 | async-start | bytes 12288 | tf_op jit(solution)/shard_map/all_to_all | solution.py:124
  37.2 17.8 %copy-start.37 = (s32[4]{0:T(128)}, s32[4]{0:T(128)S(1)}, u32[]{:S(2)}) copy-start(s32[4]{0:T(128)S(1)} %add_bitcast_fusion) | copy-start | bytes 52
  42.5 8.8 %all-to-all-start.2 = ((bf16[4,2,384]{2,1,0:T(2,128)(2,1)}), bf16[4,2,384]{2,1,0:T(2,128)(2,1)S(1)}, u32[]{:S(2)}, u32[]{:S(2)}) async-start(bf16[4,2,384]{2,1,0:T(2,128)(2,1)} %reshape.551), calls=%async_computation.2 | async-start | bytes 12288 | tf_op jit(solution)/shard_map/all_to_all | solution.py:123
  45.9 9.1 %copy-start.35 = (pred[4]{0:T(512)(128)(4,1)}, pred[4]{0:T(512)(128)(4,1)S(1)}, u32[]{:S(2)}) copy-start(pred[4]{0:T(512)(128)(4,1)S(1)} %compare_reduce_fusion) | copy-start | bytes 16
  51.3 12.5 %all-to-all-start.3 = ((bf16[4,2,16384]{2,1,0:T(2,128)(2,1)}), bf16[4,2,16384]{2,1,0:T(2,128)(2,1)S(1)}, u32[]{:S(2)}, u32[]{:S(2)}) async-start(bf16[4,2,16384]{2,1,0:T(2,128)(2,1)} %reshape.555), calls=%async_computation.3 | async-start | bytes 524288 | tf_op jit(solution)/shard_map/all_to_all | solution.py:122
  56.8 2.1 %copy-start.3 = (f32[2,128,128]{2,1,0:T(8,128)}, f32[2,128,128]{2,1,0:T(8,128)S(1)}, u32[]{:S(2)}) copy-start(f32[2,128,128]{2,1,0:T(8,128)S(1)} %fusion.46) | copy-start | bytes 393220
  56.8 0.7 copy-start.42
  59.2 0.9 copy-start.4
  59.2 0.9 copy-start.6
  59.2 0.9 copy-start.12
  59.3 0.9 copy-start.29
  59.3 0.9 copy-start.33
  59.4 0.8 copy-start.14
  61.4 0.7 copy-start.27
  64.4 0.7 copy-start.36
  64.4 0.7 copy-start.38
  65.4 0.7 copy-start.8
  69.4 0.7 copy-start.10
  69.5 0.7 copy-start.24
  69.5 0.7 copy-start.26
  71.0 0.7 copy-start.44
  71.9 0.7 copy-start.20
  71.9 0.7 copy-start.22
  73.6 29.8 %all-to-all-start.4 = ((f32[8,32,256]{2,1,0:T(8,128)}), f32[8,32,256]{2,1,0:T(8,128)S(1)}, u32[]{:S(2)}, u32[]{:S(2)}) async-start(f32[8,32,256]{2,1,0:T(8,128)} %bitcast.44), calls=%async_computation.4 | async-start | bytes 524288 | tf_op jit(solution)/shard_map/all_to_all | solution.py:181
  (2 other events, 1.3 us)
